TPU v7x, 32 devices: a whole 2x2x4 slice. The times are simulated.
32 devices in a mesh: sample: 4 (over x, core), ctx: 8 (over z, y).
Axes of the slice: x: 2, y: 2, z: 4, core: 2. Of those that a mesh axis runs over, the one named last changes fastest.
Arguments:
- queries: bfloat16 [4096, 2048], P(('sample', 'ctx')), may hold values from -4 to 4
- experts: int32 [4096, 16], P(('sample', 'ctx')), may hold values from 0 to 63, all different within a row; in each aligned block of 128 rows (0 to 127, 128 to 255, ...) at most 64 rows name the same one
- gate: float32 [4096, 16], P(('sample', 'ctx')), may hold values from 0.05 to 1
- prefix_keys: bfloat16 [128, 1024], P('ctx'), may hold values from -8 to 8
- prefix_values: bfloat16 [128, 1024], P('ctx'), may hold values from -6 to 6
- d_out: bfloat16 [4096, 2048], P(('sample', 'ctx')), may hold values from -6 to 6
- lengths: int32 [4], replicated, may hold values from 128 to 1024
Outputs:
- attended: bfloat16 [4096, 2048], P(('sample', 'ctx'))
- query_grad: bfloat16 [4096, 2048], P(('sample', 'ctx'))
- gate_grad: float32 [4096, 16], P(('sample', 'ctx'))
- key_grad: float32 [128, 1024], P('ctx')
- value_grad: float32 [128, 1024], P('ctx')
Inputs may be any that keep to these rules, and one draw needn't show every extreme that they name: `experts`: among the tokens of one device (aligned blocks of 128 tokens) no expert is picked more than 64 times, and some expert is picked exactly 64 times; a token's picks are distinct. Completion c holds tokens c * 1024 to (c + 1) * 1024 - 1; its first lengths[c] tokens are live.
All inputs are finite; a program needn't handle non-finite values.
Results may differ from a plain program's by a relative error of at most 0.012.
Values may be sent and summed in bfloat16 or wider, within the bound.
No kernel may reach another device: no remote copies, remote signals or barrier semaphores. Data moves between devices by JAX's collectives and lax.ppermute only.
A program may use at most 64 MiB of HBM per device.

v0:
```python
import jax
import jax.numpy as jnp
from jax import lax
from jax.sharding import PartitionSpec as P

HEAD = 128
KV_HEADS = 8
EXPERTS = 64
TOPK = 16
CLEN = 1024
CAP = 64


def slot_index(experts):
    flat = experts.reshape(-1)
    picked = (flat[:, None] == jnp.arange(EXPERTS, dtype=jnp.int32)[None, :]).astype(jnp.int32)
    before = jnp.cumsum(picked, axis=0) - picked
    return flat * CAP + jnp.sum(before * picked, axis=1)


def over_blocks(step, carry, pieces, start):
    keys, values = pieces
    length = keys.shape[0]
    if length > 128 and length % 128 == 0:

        def inner(state, number):
            begin = number * 128
            key_block = lax.dynamic_slice_in_dim(keys, begin, 128, 0)
            value_block = lax.dynamic_slice_in_dim(values, begin, 128, 0)
            return (step(state, key_block, value_block, start + begin), None)

        carry, _ = lax.scan(inner, carry, jnp.arange(length // 128, dtype=jnp.int32))
        return carry
    return step(carry, keys, values, start)


def local(queries, experts, gate, prefix_keys, prefix_values, d_out, lengths):
    scale = HEAD ** (-0.5)
    width = KV_HEADS * HEAD
    group = EXPERTS * CAP // KV_HEADS
    rows = queries.shape[0]
    n_ctx = lax.axis_size("ctx")
    prefix_total = prefix_keys.shape[0] * n_ctx
    block = lax.axis_index("sample") * n_ctx + lax.axis_index("ctx")
    token_ids = block * rows + jnp.arange(rows, dtype=jnp.int32)
    owners = (token_ids // CLEN)[:, None] == jnp.arange(lengths.shape[0], dtype=jnp.int32)[None, :]
    chosen = jnp.sum(jnp.where(owners, lengths[None, :], 0), axis=1)
    live = (token_ids % CLEN < chosen).astype(jnp.float32)
    slots = slot_index(experts)
    q_buf = jnp.zeros((EXPERTS * CAP, HEAD), jnp.bfloat16).at[slots].set(queries.reshape(-1, HEAD))
    q_buf = q_buf.reshape(KV_HEADS, group, HEAD)

    def scores_of(key_block):
        heads = key_block.reshape(-1, KV_HEADS, HEAD)
        return jnp.einsum("hgd,phd->hgp", q_buf, heads, preferred_element_type=jnp.float32) * scale

    def forward_step(carry, key_block, value_block, start):
        high, total, accum = carry
        score = scores_of(key_block)
        new_high = jnp.maximum(high, jnp.max(score, axis=2))
        shrink = jnp.exp(high - new_high)
        weight = jnp.exp(score - new_high[..., None])
        total = total * shrink + jnp.sum(weight, axis=2)
        heads = value_block.reshape(-1, KV_HEADS, HEAD)
        accum = accum * shrink[..., None] + jnp.einsum(
            "hgp,phd->hgd", weight.astype(jnp.bfloat16), heads, preferred_element_type=jnp.float32
        )
        return (new_high, total, accum)

    start_state = (
        jnp.full((KV_HEADS, group), -1e30, jnp.float32),
        jnp.zeros((KV_HEADS, group), jnp.float32),
        jnp.zeros((KV_HEADS, group, HEAD), jnp.float32),
    )
    high, total, accum = over_blocks(
        forward_step,
        start_state,
        (
            lax.all_gather(prefix_keys, "ctx", axis=0, tiled=True),
            lax.all_gather(prefix_values, "ctx", axis=0, tiled=True),
        ),
        jnp.int32(0),
    )
    output = accum / total[..., None]
    lse = high + jnp.log(total)
    o_rows = output.reshape(EXPERTS * CAP, HEAD)[slots].reshape(rows, TOPK, HEAD)
    cot = d_out.astype(jnp.float32).reshape(rows, TOPK, HEAD)
    factor = gate * live[:, None]
    attended = (factor[..., None] * o_rows).reshape(rows, TOPK * HEAD).astype(jnp.bfloat16)
    gate_grad = live[:, None] * jnp.sum(o_rows * cot, axis=2)
    dout_rows = (factor[..., None] * cot).astype(jnp.bfloat16)
    dout_buf = (
        jnp.zeros((EXPERTS * CAP, HEAD), jnp.bfloat16).at[slots].set(dout_rows.reshape(-1, HEAD))
    )
    dout_buf = dout_buf.reshape(KV_HEADS, group, HEAD)
    delta = jnp.sum(dout_buf.astype(jnp.float32) * output, axis=2)

    def backward_step(carry, key_block, value_block, start):
        dq_accum, grads = carry
        key_heads = key_block.reshape(-1, KV_HEADS, HEAD)
        value_heads = value_block.reshape(-1, KV_HEADS, HEAD)
        prob = jnp.exp(scores_of(key_block) - lse[..., None])
        dprob = jnp.einsum(
            "hgd,phd->hgp", dout_buf, value_heads, preferred_element_type=jnp.float32
        )
        dscore = (prob * (dprob - delta[..., None])).astype(jnp.bfloat16)
        dq_accum = (
            dq_accum
            + jnp.einsum("hgp,phd->hgd", dscore, key_heads, preferred_element_type=jnp.float32)
            * scale
        )
        key_part = (
            jnp.einsum("hgp,hgd->phd", dscore, q_buf, preferred_element_type=jnp.float32) * scale
        )
        value_part = jnp.einsum(
            "hgp,hgd->phd", prob.astype(jnp.bfloat16), dout_buf, preferred_element_type=jnp.float32
        )
        joined = jnp.concatenate(
            [key_part.reshape(-1, width), value_part.reshape(-1, width)], axis=1
        )
        grads = lax.dynamic_update_slice_in_dim(grads, joined, start, 0)
        return (dq_accum, grads)

    back_state = (
        jnp.zeros((KV_HEADS, group, HEAD), jnp.float32),
        jnp.zeros((prefix_total, 2 * width), jnp.float32),
    )
    dq_buf, grads = over_blocks(
        backward_step,
        back_state,
        (
            lax.all_gather(prefix_keys, "ctx", axis=0, tiled=True),
            lax.all_gather(prefix_values, "ctx", axis=0, tiled=True),
        ),
        jnp.int32(0),
    )
    query_grad = (
        dq_buf.reshape(EXPERTS * CAP, HEAD)[slots].reshape(rows, TOPK * HEAD).astype(jnp.bfloat16)
    )
    share = lax.psum_scatter(grads, "ctx", scatter_dimension=0, tiled=True)
    summed = lax.psum(share, "sample")
    return (attended, query_grad, gate_grad, summed[:, :width], summed[:, width:])


def solution(mesh):
    placed = (
        P(("sample", "ctx"), None),
        P(("sample", "ctx"), None),
        P(("sample", "ctx"), None),
        P("ctx", None),
        P("ctx", None),
        P(("sample", "ctx"), None),
        P(),
    )
    return jax.shard_map(
        local,
        mesh=mesh,
        in_specs=placed,
        out_specs=(
            P(("sample", "ctx"), None),
            P(("sample", "ctx"), None),
            P(("sample", "ctx"), None),
            P("ctx", None),
            P("ctx", None),
        ),
        check_vma=False,
    )
```

profile of v0, /device:TPU:0, one launch (start us, length us, event | category | flops | bytes accessed | tf_op | source)
XLA Modules:
  0.0 241.1 jit_solution(4302260018361914511)
XLA Ops:
  7.2 0.0 reduce-scatter.2.cloned.1.call-start
  7.2 0.7 broadcast_multiply_fusion.2
  7.9 0.8 copy.73
  8.7 0.1 eq.47
  8.8 0.1 eq.43
  8.9 0.7 select_reduce_fusion
  9.6 0.6 compare_convert_fusion
  10.2 0.1 copy.72
  10.3 0.1 mul.100
  10.4 1.4 copy.71
  11.8 32.8 %all_gather.8 = bf16[128,1024]{1,0:T(8,128)(2,1)S(1)} all-gather(bf16[16,1024]{1,0:T(8,128)(2,1)} %param.10), channel_id=1, replica_groups=mesh['sample'=4,'ctx'=8] {'ctx'}, dimensions={0}, use_global_device_ids=true | all-gather | bytes 294912 | tf_op jit(solution)/shard_map/all_gather | solution.py:79
  44.6 0.2 copy.77
  44.7 31.0 %all_gather.9 = bf16[128,1024]{1,0:T(8,128)(2,1)S(1)} all-gather(bf16[16,1024]{1,0:T(8,128)(2,1)} %param.11), channel_id=1, replica_groups=mesh['sample'=4,'ctx'=8] {'ctx'}, dimensions={0}, use_global_device_ids=true | all-gather | bytes 294912 | tf_op jit(solution)/shard_map/all_gather | solution.py:80
  75.7 0.8 copy.79
  76.6 0.0 copy-start.10
  76.6 18.1 %reduce-window.6 = s32[64,16,128]{2,1,0:T(8,128)S(1)} reduce-window(s32[64,16,128]{2,1,0:T(8,128)S(1)} %fusion.17, s32[]{:T(128)} %constant.50.clone.1), window={size=1x1x128 pad=0_0x0_0x127_0}, to_apply=%region_1.2 | reduce-window | flops 16646144 | bytes 1048580 | tf_op jit(solution)/shard_map/reduce-window
  94.7 0.2 slice.20
  94.9 0.4 copy.107
  95.4 0.2 reduce-window.9
  95.6 0.2 broadcast_add_fusion
  95.8 0.3 fusion.12
  96.1 0.0 copy-start.13
  96.1 0.0 copy-done.10
  96.1 0.0 copy-start.11
  96.1 1.0 reshape.198
  97.1 0.2 reshape.177
  97.4 6.6 %scatter_custom_fusion = bf16[4096,128]{1,0:T(8,128)(2,1)S(1)} fusion(s32[2048]{0:T(1024)S(1)} %bitcast.70, bf16[2048,128]{1,0:T(8,128)(2,1)} %reshape.198, bf16[]{:T(256)} %constant.57.clone.1), kind=kCustom, calls=%fused_computation.32 | custom fusion | bytes 1049088 | tf_op jit(solution)/shard_map/scatter | solution.py:50
  104.0 0.0 copy-start.7
  104.0 0.5 fusion.20
  104.5 0.3 fusion
  104.8 0.1 copy-done.3
  104.9 0.2 copy-done.7
  105.1 2.3 add_divide_fusion
  107.4 7.6 %gather_fusion = f32[2048,128]{1,0:T(8,128)} fusion(f32[4096,128]{1,0:T(8,128)S(1)} %bitcast.51, s32[2048]{0:T(1024)S(1)} %broadcast_clamp_fusion), kind=kCustom, calls=%fused_computation | custom fusion | bytes 2105344 | tf_op jit(solution)/shard_map/gather | solution.py:86
  115.0 1.6 multiply_reduce_fusion.1
  116.5 0.1 reduce_sum.55
  116.6 0.9 broadcast_multiply_fusion
  117.6 0.7 mul.105
  118.2 7.4 %scatter_custom_fusion.1 = bf16[4096,128]{1,0:T(8,128)(2,1)S(1)} fusion(s32[2048]{0:T(1024)} %bitcast.71, f32[2048,128]{1,0:T(8,128)} %copy-done.2, f32[2048]{0:T(1024)} %mul.105, bf16[]{:T(256)} %constant.57.clone.1), kind=kCustom, calls=%fused_computation.23 | custom fusion | flops 524288 | bytes 2105856 | tf_op jit(solution)/shard_map/scatter | solution.py:93
  125.7 0.6 multiply_reduce_fusion
  126.3 0.0 copy-start.8
  126.3 0.9 copy-done.1
  127.2 1.4 fusion.3
  128.7 0.6 multiply_convert_fusion
  129.3 0.6 copy-done.4
  129.9 0.5 convolution_multiply_fusion.2
  130.4 1.0 copy.92
  131.4 0.2 copy.93
  131.6 2.2 pad_maximum_fusion
  133.8 0.0 reduce-scatter.2.cloned.1.call-update
  133.9 0.0 all-reduce.2.cloned.1.call-start
  133.9 0.2 reshape.169
  134.1 0.3 mul.96
  134.4 1.2 fusion.6
  135.6 64.0 %reduce-scatter.2.cloned.1.call-done = f32[16,2048]{1,0:T(8,128)} async-done(((f32[128,2048]{1,0:T(8,128)}), f32[16,2048]{1,0:T(8,128)}) %reduce-scatter.2.cloned.1.call-update) | async-done | bytes 131088 | tf_op jit(solution)/shard_map/reduce_scatter | solution.py:140
  199.6 0.0 all-reduce.2.cloned.1.call-update
  199.6 0.0 copy-start.12
  199.6 0.4 convolution_multiply_fusion
  200.1 0.7 copy.94
  200.7 0.7 copy.87
  201.4 6.2 %gather_fusion.1 = bf16[2048,128]{1,0:T(8,128)(2,1)S(1)} fusion(bf16[4096,128]{1,0:T(8,128)(2,1)S(1)} %bitcast.52, s32[2048]{0:T(1024)S(1)} %copy-done.12), kind=kCustom, calls=%fused_computation.1 | custom fusion | bytes 1056768 | tf_op jit(solution)/shard_map/gather | solution.py:138
  207.6 1.0 convert_element_type.49
  208.6 24.1 %all-reduce.2.cloned.1.call-done = f32[16,2048]{1,0:T(8,128)} async-done(((f32[16,2048]{1,0:T(8,128)}), f32[16,2048]{1,0:T(8,128)}) %all-reduce.2.cloned.1.call-update) | async-done | bytes 131088 | tf_op jit(solution)/shard_map/psum | solution.py:141
  232.7 1.5 fusion.19
  (23 shorter events, 0.1 us)
Async XLA Ops:
  7.2 192.4 %reduce-scatter.2.cloned.1.call-start = ((), (), s32[]{:S(2)}) async-start(), calls=%async_computation.1 | async-start | bytes 1179648 | tf_op jit(solution)/shard_map/reduce_scatter | solution.py:140
  76.6 19.5 %copy-start.10 = (bf16[128,2048]{1,0:T(8,128)(2,1)S(1)}, bf16[128,2048]{1,0:T(8,128)(2,1)}, u32[]{:S(2)}) copy-start(bf16[128,2048]{1,0:T(8,128)(2,1)} %param.7) | copy-start | bytes 1572868
  94.7 2.4 %copy-start.9 = (bf16[128,2048]{1,0:T(8,128)(2,1)S(1)}, bf16[128,2048]{1,0:T(8,128)(2,1)}, u32[]{:S(2)}) copy-start(bf16[128,2048]{1,0:T(8,128)(2,1)} %param.12) | copy-start | bytes 1572868
  96.1 7.9 %copy-start.13 = (s32[2048,1]{0,1:T(1,128)}, s32[2048,1]{0,1:T(1,128)S(1)}, u32[]{:S(2)}) copy-start(s32[2048,1]{0,1:T(1,128)S(1)} %compare_select_fusion) | copy-start | bytes 24580
  96.1 11.3 %copy-start.11 = (s32[2048]{0:T(1024)}, s32[2048]{0:T(1024)S(1)}, u32[]{:S(2)}) copy-start(s32[2048]{0:T(1024)S(1)} %broadcast_clamp_fusion) | copy-start | bytes 24580
  97.3 17.6 %copy-start.2 = (f32[2048,128]{1,0:T(8,128)}, f32[2048,128]{1,0:T(8,128)S(1)}, u32[]{:S(2)}) copy-start(f32[2048,128]{1,0:T(8,128)S(1)} %reshape.177) | copy-start | bytes 3145732
  103.9 1.0 copy-start.3
  104.0 1.2 copy-start.7
  104.5 2.9 %copy-start = (f32[8,512,128]{1,2,0:T(8,128)}, f32[8,512,128]{1,2,0:T(8,128)S(1)}, u32[]{:S(2)}) copy-start(f32[8,512,128]{1,2,0:T(8,128)S(1)} %get-tuple-element.28) | copy-start | bytes 6291460
  125.6 1.6 copy-start.1
  126.3 2.4 copy-start.8
  128.7 1.2 copy-start.4
  129.9 1.5 copy-start.6
  131.4 2.5 %copy-start.5 = (f32[2048,128]{1,0:T(8,128)S(1)}, f32[2048,128]{1,0:T(8,128)}, u32[]{:S(2)}) copy-start(f32[2048,128]{1,0:T(8,128)} %gather_fusion) | copy-start | bytes 3145732
  133.9 98.9 %all-reduce.2.cloned.1.call-start = ((), (), s32[]{:S(2)}) async-start(), calls=%async_computation.2 | async-start | bytes 262144 | tf_op jit(solution)/shard_map/psum | solution.py:141
  199.6 1.8 copy-start.12
Sparse Core Ops, SparseCore 0:
  134.0 65.5 reduce-scatter.1
  201.9 30.7 all-reduce.1
where the time goes:
time: 242 us; the launch traced here: 241 us
  waiting for transfers between devices  88.2 us (36%)
  blocking collectives  63.7 us (26%)
  other arithmetic  35.1 us (15%)
  local copies, waits for them, and re-layouts  34 us (14%)
  between operations  14.4 us (6%)
  matrix products  5.69 us (2%)
    reduce_scatter x1, waiting for transfers between devices, local(): share = lax.psum_scatter(grads, 'ctx', scatter_dimension=0, tiled=True)  64 us
    all_gather x1, blocking collectives, local(): lax.all_gather(prefix_keys, 'ctx', axis=0, tiled=True)  32.8 us
    all_gather x1, blocking collectives, local(): lax.all_gather(prefix_values, 'ctx', axis=0, tiled=True)  31 us
    psum x1, waiting for transfers between devices, local(): summed = lax.psum(share, 'sample')  24.1 us
    another operation x3, other arithmetic  18.5 us
    gather x1, local copies, waits for them, and re-layouts, local(): output.reshape(EXPERTS * CAP, HEAD)[slots].reshape(rows, TOPK, HEAD)  7.56 us
    scatter x1, other arithmetic, local(): jnp.zeros((EXPERTS * CAP, HEAD), jnp.bfloat16).at[slots]  7.39 us
    scatter x1, local copies, waits for them, and re-layouts, local(): jnp.zeros((EXPERTS * CAP, HEAD), jnp.bfloat16).at[slots]  6.57 us
  transfers between devices with their start and end apart: 2, of which 2 were waited for; matrix products, arithmetic and copies ran while one was open for 4% of the time, Pallas kernels for 0%

commit v1 on v0

--- a/solution.py
+++ b/solution.py
@@ -138,7 +138,7 @@
         dq_buf.reshape(EXPERTS * CAP, HEAD)[slots].reshape(rows, TOPK * HEAD).astype(jnp.bfloat16)
     )
     share = lax.psum_scatter(grads, "ctx", scatter_dimension=0, tiled=True)
-    summed = lax.psum(share, "sample")
+    summed = jnp.sum(lax.all_gather(share, "sample"), axis=0)
     return (attended, query_grad, gate_grad, summed[:, :width], summed[:, width:])
 
 

time: 242 us -> 214 us (0.88)
  waiting for transfers between devices: 88.2 us -> 54.5 us
  blocking collectives: 63.7 us -> 71.1 us
    psum x1 -> x0, waiting for transfers between devices: 24.1 us -> none  [local(): summed = lax.psum(share, 'sample')]
    reduce_scatter x1, waiting for transfers between devices: 64 us -> 54.5 us  [local(): share = lax.psum_scatter(grads, 'ctx', scatter_dimension=0, tiled=True)]
    all_gather x0 -> x1, blocking collectives: none -> 7.34 us  [local(): summed = jnp.sum(lax.all_gather(share, 'sample'), axis=0)]
  transfers between devices with their start and end apart: 2 -> 1, of which waited for: 2 -> 1; matrix products, arithmetic and copies ran while one was open for 4% -> 5% of each run, Pallas kernels for 0% -> 0%
where the time goes in v1:
time: 214 us
  blocking collectives  71.1 us (33%)
  waiting for transfers between devices  54.5 us (25%)
  other arithmetic  35.8 us (17%)
  local copies, waits for them, and re-layouts  32.5 us (15%)
  between operations  14.3 us (7%)
  matrix products  5.69 us (3%)
    reduce_scatter x1, waiting for transfers between devices, local(): share = lax.psum_scatter(grads, 'ctx', scatter_dimension=0, tiled=True)  54.5 us
    all_gather x1, blocking collectives, local(): lax.all_gather(prefix_keys, 'ctx', axis=0, tiled=True)  32.8 us
    all_gather x1, blocking collectives, local(): lax.all_gather(prefix_values, 'ctx', axis=0, tiled=True)  31 us
    another operation x3, other arithmetic  18.5 us
    scatter x1, other arithmetic, local(): jnp.zeros((EXPERTS * CAP, HEAD), jnp.bfloat16).at[slots]  7.62 us
    gather x1, local copies, waits for them, and re-layouts, local(): output.reshape(EXPERTS * CAP, HEAD)[slots].reshape(rows, TOPK, HEAD)  7.56 us
    all_gather x1, blocking collectives, local(): summed = jnp.sum(lax.all_gather(share, 'sample'), axis=0)  7.34 us
    scatter x1, local copies, waits for them, and re-layouts, local(): jnp.zeros((EXPERTS * CAP, HEAD), jnp.bfloat16).at[slots]  6.57 us
  transfers between devices with their start and end apart: 1, of which 1 were waited for; matrix products, arithmetic and copies ran while one was open for 5% of the time, Pallas kernels for 0%

profile of v1, /device:TPU:0, one launch (start us, length us, event | category | flops | bytes accessed | tf_op | source)
XLA Modules:
  0.0 213.9 jit_solution(6854697959179428661)
XLA Ops:
  7.2 0.0 reduce-scatter.2.cloned.1.call-start
  7.2 0.7 broadcast_multiply_fusion.2
  7.9 0.8 copy.71
  8.7 0.1 eq.47
  8.8 0.1 eq.43
  8.9 0.7 select_reduce_fusion
  9.6 0.6 compare_convert_fusion
  10.2 0.1 copy.70
  10.3 0.1 mul.100
  10.4 0.8 copy.69
  11.2 32.8 %all_gather.14 = bf16[128,1024]{1,0:T(8,128)(2,1)S(1)} all-gather(bf16[16,1024]{1,0:T(8,128)(2,1)} %param.10), channel_id=1, replica_groups=mesh['sample'=4,'ctx'=8] {'ctx'}, dimensions={0}, use_global_device_ids=true | all-gather | bytes 294912 | tf_op jit(solution)/shard_map/all_gather | solution.py:79
  43.9 0.2 copy.75
  44.1 31.0 %all_gather.15 = bf16[128,1024]{1,0:T(8,128)(2,1)S(1)} all-gather(bf16[16,1024]{1,0:T(8,128)(2,1)} %param.11), channel_id=1, replica_groups=mesh['sample'=4,'ctx'=8] {'ctx'}, dimensions={0}, use_global_device_ids=true | all-gather | bytes 294912 | tf_op jit(solution)/shard_map/all_gather | solution.py:80
  75.1 0.8 copy.77
  76.0 0.0 copy-start.10
  76.0 18.1 %reduce-window.6 = s32[64,16,128]{2,1,0:T(8,128)S(1)} reduce-window(s32[64,16,128]{2,1,0:T(8,128)S(1)} %fusion.17, s32[]{:T(128)} %constant.50.clone.1), window={size=1x1x128 pad=0_0x0_0x127_0}, to_apply=%region_1.2 | reduce-window | flops 16646144 | bytes 1048580 | tf_op jit(solution)/shard_map/reduce-window
  94.1 0.2 slice.20
  94.3 0.4 copy.105
  94.7 0.2 reduce-window.9
  94.9 0.2 broadcast_add_fusion
  95.2 0.3 fusion.12
  95.4 0.0 copy-start.14
  95.5 0.0 copy-done.10
  95.5 0.0 copy-start.12
  95.5 1.0 reshape.198
  96.5 0.0 copy-done.9
  96.5 0.2 reshape.177
  96.7 6.6 %scatter_custom_fusion = bf16[4096,128]{1,0:T(8,128)(2,1)S(1)} fusion(s32[2048]{0:T(1024)S(1)} %bitcast.72, bf16[2048,128]{1,0:T(8,128)(2,1)} %reshape.198, bf16[]{:T(256)} %constant.57.clone.1), kind=kCustom, calls=%fused_computation.32 | custom fusion | bytes 1049088 | tf_op jit(solution)/shard_map/scatter | solution.py:50
  103.3 0.0 copy-start.7
  103.3 0.5 fusion.20
  103.9 0.3 fusion
  104.2 0.1 copy-done.3
  104.3 0.2 copy-done.7
  104.5 2.3 %add_divide_fusion = f32[8,512,128]{2,1,0:T(8,128)S(1)} fusion(bf16[128,8,128]{0,2,1:T(8,128)(2,1)S(1)} %bitcast.66, f32[8,512,128]{1,2,0:T(8,128)S(1)} %get-tuple-element.28, f32[8,512]{1,0:T(8,128)S(1)} %get-tuple-element.23, f32[8,512]{1,0:T(8,128)S(1)} %broadcast_maximum_fusion, f32[8,512]{1,0:T(8,128)S(1)} %get-tuple-element.24), kind=kOutput, calls=%fused_computation.7 | convolution fusion | flops 136314880 | bytes 4505600 | tf_op jit(solution)/shard_map/hgp,phd->hgd/dot_general | solution.py:65
  106.8 7.6 %gather_fusion = f32[2048,128]{1,0:T(8,128)} fusion(f32[4096,128]{1,0:T(8,128)S(1)} %bitcast.52, s32[2048]{0:T(1024)S(1)} %broadcast_clamp_fusion), kind=kCustom, calls=%fused_computation | custom fusion | bytes 2105344 | tf_op jit(solution)/shard_map/gather | solution.py:86
  114.4 1.6 multiply_reduce_fusion.1
  115.9 0.1 reduce_sum.64
  116.0 1.3 broadcast_multiply_fusion
  117.4 0.1 mul.105
  117.4 7.6 %scatter_custom_fusion.1 = bf16[4096,128]{1,0:T(8,128)(2,1)S(1)} fusion(s32[2048]{0:T(1024)} %bitcast.73, f32[2048,128]{1,0:T(8,128)} %copy-done.2, f32[2048]{0:T(1024)S(1)} %mul.105, bf16[]{:T(256)} %constant.57.clone.1), kind=kCustom, calls=%fused_computation.23 | custom fusion | flops 524288 | bytes 2105856 | tf_op jit(solution)/shard_map/scatter | solution.py:93
  125.1 0.6 multiply_reduce_fusion
  125.7 0.0 copy-start.8
  125.7 0.9 copy-done.1
  126.7 1.4 fusion.3
  128.1 0.6 multiply_convert_fusion
  128.7 0.6 copy-done.4
  129.3 0.5 convolution_multiply_fusion.2
  129.8 1.0 copy.90
  130.8 0.2 copy.91
  131.0 2.2 %pad_maximum_fusion = f32[128,2048]{1,0:T(8,128)} fusion(f32[128,1024]{1,0:T(8,128)S(1)} %copy.91, f32[128,1024]{1,0:T(8,128)} %copy.90), kind=kLoop, calls=%fused_computation.18 | loop fusion | flops 262144 | bytes 2097152 | tf_op jit(solution)/shard_map/concatenate | solution.py:118
  133.3 0.0 reduce-scatter.2.cloned.1.call-update
  133.3 0.0 copy-done.5
  133.3 0.2 reshape.169
  133.5 0.6 copy-done.11
  134.1 0.7 copy.92
  134.8 0.4 convolution_multiply_fusion
  135.2 0.7 copy.85
  135.9 6.2 %gather_fusion.1 = bf16[2048,128]{1,0:T(8,128)(2,1)S(1)} fusion(bf16[4096,128]{1,0:T(8,128)(2,1)S(1)} %bitcast.53, s32[2048]{0:T(1024)S(1)} %copy-done.13), kind=kCustom, calls=%fused_computation.1 | custom fusion | bytes 1056768 | tf_op jit(solution)/shard_map/gather | solution.py:138
  142.1 1.0 convert_element_type.49
  143.1 0.3 mul.96
  143.4 1.2 fusion.6
  144.6 54.5 %reduce-scatter.2.cloned.1.call-done = f32[16,2048]{1,0:T(8,128)} async-done(((f32[128,2048]{1,0:T(8,128)}), f32[16,2048]{1,0:T(8,128)}) %reduce-scatter.2.cloned.1.call-update) | async-done | bytes 131088 | tf_op jit(solution)/shard_map/reduce_scatter | solution.py:140
  199.0 7.3 %all-gather = f32[64,2048]{1,0:T(8,128)S(1)} all-gather(f32[16,2048]{1,0:T(8,128)} %reduce-scatter.2.cloned.1.call-done), channel_id=2, replica_groups=mesh['sample'=4,'ctx'=8] {'sample'}, dimensions={0}, use_global_device_ids=true | all-gather | bytes 655360 | tf_op jit(solution)/shard_map/all_gather | solution.py:141
  206.4 0.7 fusion.19
  (24 shorter events, 0.1 us)
Async XLA Ops:
  7.2 191.9 %reduce-scatter.2.cloned.1.call-start = ((), (), s32[]{:S(2)}) async-start(), calls=%async_computation.1 | async-start | bytes 1179648 | tf_op jit(solution)/shard_map/reduce_scatter | solution.py:140
  76.0 19.5 %copy-start.10 = (bf16[128,2048]{1,0:T(8,128)(2,1)S(1)}, bf16[128,2048]{1,0:T(8,128)(2,1)}, u32[]{:S(2)}) copy-start(bf16[128,2048]{1,0:T(8,128)(2,1)} %param.7) | copy-start | bytes 1572868
  94.1 2.4 %copy-start.9 = (bf16[128,2048]{1,0:T(8,128)(2,1)S(1)}, bf16[128,2048]{1,0:T(8,128)(2,1)}, u32[]{:S(2)}) copy-start(bf16[128,2048]{1,0:T(8,128)(2,1)} %param.12) | copy-start | bytes 1572868
  95.4 7.9 %copy-start.14 = (s32[2048,1]{0,1:T(1,128)}, s32[2048,1]{0,1:T(1,128)S(1)}, u32[]{:S(2)}) copy-start(s32[2048,1]{0,1:T(1,128)S(1)} %compare_select_fusion) | copy-start | bytes 24580
  95.5 11.3 %copy-start.12 = (s32[2048]{0:T(1024)}, s32[2048]{0:T(1024)S(1)}, u32[]{:S(2)}) copy-start(s32[2048]{0:T(1024)S(1)} %broadcast_clamp_fusion) | copy-start | bytes 24580
  96.7 17.6 %copy-start.2 = (f32[2048,128]{1,0:T(8,128)}, f32[2048,128]{1,0:T(8,128)S(1)}, u32[]{:S(2)}) copy-start(f32[2048,128]{1,0:T(8,128)S(1)} %reshape.177) | copy-start | bytes 3145732
  103.3 1.0 copy-start.3
  103.3 1.2 copy-start.7
  103.8 2.9 %copy-start = (f32[8,512,128]{1,2,0:T(8,128)}, f32[8,512,128]{1,2,0:T(8,128)S(1)}, u32[]{:S(2)}) copy-start(f32[8,512,128]{1,2,0:T(8,128)S(1)} %get-tuple-element.28) | copy-start | bytes 6291460
  125.1 1.6 copy-start.1
  125.7 2.4 %copy-start.8 = (bf16[128,1024]{0,1:T(8,128)(2,1)S(1)}, bf16[128,1024]{0,1:T(8,128)(2,1)}, u32[]{:S(2)}) copy-start(bf16[128,1024]{0,1:T(8,128)(2,1)} %copy.77) | copy-start | bytes 786436
  128.1 1.2 copy-start.4
  129.3 1.5 copy-start.6
  130.8 2.5 %copy-start.5 = (f32[2048,128]{1,0:T(8,128)S(1)}, f32[2048,128]{1,0:T(8,128)}, u32[]{:S(2)}) copy-start(f32[2048,128]{1,0:T(8,128)} %gather_fusion) | copy-start | bytes 3145732
  133.3 0.8 copy-start.11
  134.8 1.1 copy-start.13
Sparse Core Ops, SparseCore 0:
  133.4 65.5 reduce-scatter.1
